TPU v7x, 512 devices: a whole 4x8x8 slice. The times are simulated.
512 devices in a mesh: box: 64 (over y, x, core), samp: 8 (over z).
Axes of the slice: x: 4, y: 8, z: 8, core: 2. Of those that a mesh axis runs over, the one named last changes fastest.
Arguments:
- currents: bfloat16 [2048, 8, 128], P(('box', 'samp')), may hold values from -6 to 6
- radiation: bfloat16 [2048, 2, 2, 512, 128], P(('box', 'samp')), may hold values from -0.1875 to 0.1875
- near_blocks: bfloat16 [2048, 8, 2, 128, 128], P(('box', 'samp')), may hold values from -0.125 to 0.125
- near_src: int32 [2048, 8], P(('box', 'samp')), may hold values from 0 to 2047, as said below
- leaf_parent: int32 [2048], P('box'), may hold values from 0 to 1023, as said below
- leaf_shift: int32 [2048], P('box'), may hold values from 0 to 7
- shift_table: bfloat16 [8, 2, 8192], P(None, None, 'samp'), may hold values from -4 to 4
- interp_idx: int32 [64, 2], P('samp'), may hold values from 0 to 3, as said below
- interp_val: bfloat16 [64, 2, 128, 128], P('samp'), may hold values from -0.375 to 0.375
- top_src: int32 [1024, 16], P('box'), may hold values from 0 to 1023, as said below
- top_disp: int32 [1024, 16], P('box'), may hold values from 0 to 31
- trans_table: bfloat16 [32, 2, 8192], P(None, None, 'samp'), may hold values from -1 to 1
Outputs:
- matvec: float32 [2048, 8, 128], P(('box', 'samp'))
Inputs may be any that keep to these rules, and one draw needn't show every extreme that they name: `near_src`: entry 0 of a leaf's row is the leaf itself; every entry lies in the 4 leaves of the leaf's own device or of the devices just before and after it in box+samp order (leaves numbered box-major), and these ends are reached. `leaf_parent`: the parent of leaf l lies in its box group: its value divided by 16 equals l divided by 32. `interp_idx`: the 2 entries of a row differ. `top_src`: a source of top box t is another box of t's group (t // 16), or one of the last 8 boxes of the group before it, or one of the first 8 boxes of the group after it; both rims are reached.
All inputs are finite; a program needn't handle non-finite values.
Results may differ from a plain program's by a relative error of at most 0.013.
Values may be sent and summed in bfloat16 or wider, within the bound.
A program may use at most 64 MiB of HBM per device.

v0:
```python
import jax
import jax.numpy as jnp
from jax import lax
from jax.sharding import PartitionSpec as P

HIGHEST = lax.Precision.HIGHEST


def with_halo(cells, sides, width):
    for axis, dim in sides:
        count = lax.axis_size(axis)
        ends = count - 1
        head = lax.slice_in_dim(cells, 0, width, axis=dim)
        tail = lax.slice_in_dim(cells, cells.shape[dim] - width, cells.shape[dim], axis=dim)
        cells = jnp.concatenate(
            [
                lax.ppermute(tail, axis, [(i, (i + 1) % count) for i in range(ends)]),
                cells,
                lax.ppermute(head, axis, [((i + 1) % count, i) for i in range(ends)]),
            ],
            axis=dim,
        )
    return cells


def complex_mul(a_real, a_imag, b_real, b_imag):
    return (a_real * b_real - a_imag * b_imag, a_real * b_imag + a_imag * b_real)


def contract(form, first_op, second_op):
    return jnp.einsum(form, first_op, second_op, preferred_element_type=jnp.float32)


def per_device(
    currents,
    radiation,
    near_blocks,
    near_src,
    leaf_parent,
    leaf_shift,
    shift_table,
    interp_idx,
    interp_val,
    top_src,
    top_disp,
    trans_table,
):
    leaf_count = currents.shape[0]
    half_comp = currents.shape[1]
    excite = half_comp // 2
    comps = 2 * half_comp
    samp_count = lax.axis_size("samp")
    group_index = lax.axis_index("box")
    first_leaf = (group_index * samp_count + lax.axis_index("samp")) * leaf_count
    top_count = top_src.shape[0]
    block_size = interp_val.shape[2]
    leaf_samples = radiation.shape[3]
    in_blocks = leaf_samples // block_size
    local_blocks = interp_val.shape[0]
    local_samples = local_blocks * block_size
    neighbours = with_halo(currents, ((("box", "samp"), 0),), leaf_count)
    rad_real = radiation[:, :, 0]
    rad_imag = radiation[:, :, 1]
    form_out = "lpqu,leu->lpeq"
    out_real = contract(form_out, rad_real, currents[:, :excite]) - contract(
        form_out, rad_imag, currents[:, excite:]
    )
    out_imag = contract(form_out, rad_real, currents[:, excite:]) + contract(
        form_out, rad_imag, currents[:, :excite]
    )
    patterns = jnp.concatenate(
        [
            out_real.reshape(leaf_count, half_comp, leaf_samples),
            out_imag.reshape(leaf_count, half_comp, leaf_samples),
        ],
        axis=1,
    ).astype(jnp.bfloat16)
    piece = lax.all_gather(patterns, "samp", axis=0, tiled=True)
    piece_rows = piece.shape[0]
    picked = piece.reshape(piece_rows, comps, in_blocks, block_size)[:, :, interp_idx, :]
    moved_rows = contract("lcbri,brki->lcbk", picked, interp_val)
    moved = moved_rows.reshape(piece_rows, comps, local_samples)
    shift_onehot = (leaf_shift[:, None] == jnp.arange(shift_table.shape[0])[None, :]).astype(
        jnp.bfloat16
    )
    shift_rows = contract("ln,nrk->lrk", shift_onehot, shift_table)
    shift_real = shift_rows[:, 0:1]
    shift_imag = shift_rows[:, 1:2]
    up_real, up_imag = complex_mul(
        moved[:, :half_comp], moved[:, half_comp:], shift_real, shift_imag
    )
    shifted = jnp.concatenate([up_real, up_imag], axis=1)
    parent_local = leaf_parent - group_index * top_count
    member = parent_local[None, :] == jnp.arange(top_count)[:, None]
    top_patterns = jnp.einsum(
        "tl,lck->tck", member.astype(jnp.float32), shifted, precision=HIGHEST
    ).astype(jnp.bfloat16)
    padded = with_halo(top_patterns, (("box", 0),), top_count)
    base_index = group_index * top_count - top_count
    disp_count = trans_table.shape[0]

    def add_entry(entry, total):
        source_rows = jnp.take(padded, top_src[:, entry] - base_index, axis=0).astype(jnp.float32)
        disp_onehot = (top_disp[:, entry][:, None] == jnp.arange(disp_count)[None, :]).astype(
            jnp.bfloat16
        )
        coeff = contract("tn,nrk->trk", disp_onehot, trans_table)
        part_real, part_imag = complex_mul(
            coeff[:, 0:1], coeff[:, 1:2], source_rows[:, :half_comp], source_rows[:, half_comp:]
        )
        return total + jnp.concatenate([part_real, part_imag], axis=1)

    incoming = lax.fori_loop(
        0, top_src.shape[1], add_entry, jnp.zeros((top_count, comps, local_samples), jnp.float32)
    ).astype(jnp.bfloat16)
    spread = contract("tl,tck->lck", member.astype(jnp.bfloat16), incoming)
    down_real, down_imag = complex_mul(
        shift_real, -shift_imag, spread[:, :half_comp], spread[:, half_comp:]
    )
    down = jnp.concatenate([down_real, down_imag], axis=1).astype(jnp.bfloat16)
    block_onehot = (interp_idx[:, :, None] == jnp.arange(in_blocks)[None, None, :]).astype(
        jnp.float32
    )
    parts = contract(
        "lcbk,brki->lcbri",
        down.reshape(leaf_count * lax.axis_size("samp"), comps, local_blocks, block_size),
        interp_val,
    )
    folded = jnp.einsum("lcbri,brq->lcqi", parts, block_onehot, precision=HIGHEST)
    far = lax.psum_scatter(
        folded.reshape(leaf_count * lax.axis_size("samp"), comps, leaf_samples).astype(
            jnp.bfloat16
        ),
        "samp",
        scatter_dimension=0,
        tiled=True,
    )
    far_real = far[:, :half_comp].reshape(leaf_count, 2, excite, leaf_samples)
    far_imag = far[:, half_comp:].reshape(leaf_count, 2, excite, leaf_samples)
    form_back = "lpqu,lpeq->leu"
    recv_real = contract(form_back, rad_real, far_real) + contract(form_back, rad_imag, far_imag)
    recv_imag = contract(form_back, rad_real, far_imag) - contract(form_back, rad_imag, far_real)
    near_rows = jnp.take(neighbours, near_src - first_leaf + leaf_count, axis=0)
    block_real = near_blocks[:, :, 0]
    block_imag = near_blocks[:, :, 1]
    form_near = "lnuv,lnev->leu"
    near_real = contract(form_near, block_real, near_rows[:, :, :excite]) - contract(
        form_near, block_imag, near_rows[:, :, excite:]
    )
    near_imag = contract(form_near, block_real, near_rows[:, :, excite:]) + contract(
        form_near, block_imag, near_rows[:, :, :excite]
    )
    return jnp.concatenate([recv_real + near_real, recv_imag + near_imag], axis=1)


def solution(mesh):
    placed = (
        P(("box", "samp"), None, None),
        P(("box", "samp"), None, None, None, None),
        P(("box", "samp"), None, None, None, None),
        P(("box", "samp"), None),
        P("box"),
        P("box"),
        P(None, None, "samp"),
        P("samp", None),
        P("samp", None, None, None),
        P("box", None),
        P("box", None),
        P(None, None, "samp"),
    )
    return jax.shard_map(
        per_device,
        mesh=mesh,
        in_specs=placed,
        out_specs=P(("box", "samp"), None, None),
        check_vma=False,
    )
```

profile of v0, /device:TPU:2, one launch (start us, length us, event | category | flops | bytes accessed | tf_op | source)
XLA Modules:
  0.0 176.0 jit_solution(13195029039709390717)
XLA Ops:
  11.1 31.6 %all_gather.3 = bf16[32,16,512]{2,1,0:T(8,128)(2,1)S(1)} all-gather(bf16[4,16,512]{2,1,0:T(8,128)(2,1)S(1)} %pad_maximum_fusion.1), channel_id=1, replica_groups=mesh['box'=64,'samp'=8] {'samp'}, dimensions={0}, use_global_device_ids=true | all-gather | bytes 589824 | tf_op jit(solution)/shard_map/all_gather | solution.py:78
  44.9 2.5 %copy.92 = f32[32,16,8,128]{3,2,0,1:T(8,128)} copy(f32[32,16,8,128]{3,1,0,2:T(8,128)S(1)} %convolution_bitcast_fusion.1) | data formatting | bytes 4194304 | tf_op jit(solution)/shard_map/reshape | solution.py:82
  52.3 3.8 %collective-permute-start.1 = (bf16[16,16,1024]{2,0,1:T(8,128)(2,1)S(1)}, bf16[16,16,1024]{2,0,1:T(8,128)(2,1)}, u32[]{:S(2)}, u32[]{:S(2)}) collective-permute-start(bf16[16,16,1024]{2,0,1:T(8,128)(2,1)S(1)} %fusion.16), channel_id=1, source_target_pairs={{8,0},{16,8},{24,16},{32,24},{40,32},{48,40},{56,48},{64,56},{72,6... | collective-permute-start | bytes 1572872 | tf_op jit(solution)/shard_map/ppermute | solution.py:19
  56.3 4.5 %collective-permute-done = bf16[16,16,1024]{2,0,1:T(8,128)(2,1)S(1)} collective-permute-done((bf16[16,16,1024]{2,0,1:T(8,128)(2,1)S(1)}, bf16[16,16,1024]{2,0,1:T(8,128)(2,1)S(1)}, u32[]{:S(2)}, u32[]{:S(2)}) %collective-permute-start) | collective-permute-done | bytes 524320 | tf_op jit(solution)/shard_map/ppermute | solution.py:17
  63.8 2.0 %copy.70 = bf16[48,16,1024]{2,1,0:T(8,128)(2,1)} copy(bf16[48,16,1024]{2,0,1:T(8,128)(2,1)S(1)} %pad_maximum_fusion) | data formatting | bytes 3145728
  65.9 48.1 %while.14 = (s32[]{:T(128)}, f32[16,16,1024]{2,1,0:T(8,128)S(1)}, s32[16,16]{0,1:T(8,128)S(1)}, bf16[32,2,1024]{2,0,1:T(8,128)(2,1)S(1)}, s32[16,16]{0,1:T(8,128...) while((s32[]{:T(128)}, f32[16,16,1024]{2,1,0:T(8,128)S(1)}, ...), condition=%wide.region_1.0_spmd.clone, body=%wide.region_0.1_spmd.clone.sunk | while | flops 4195955 | bytes 8524371 | solution.py:113
  65.9 2.0 %gather_fusion = bf16[16,16,1024]{2,1,0:T(8,128)(2,1)S(1)} fusion(bf16[48,16,1024]{2,1,0:T(8,128)(2,1)} %get-tuple-element.292, s32[1024]{0:T(1024)S(1)} %pad_clamp_fusion.4), kind=kCustom, calls=%fused_computation.clone.clone.1 | custom fusion | bytes 1048640 | tf_op jit(solution)/shard_map/while/body/eval_jaxpr/jit(_take)/gather | solution.py:103
  68.9 2.0 %gather_fusion = bf16[16,16,1024]{2,1,0:T(8,128)(2,1)S(1)} fusion(bf16[48,16,1024]{2,1,0:T(8,128)(2,1)} %get-tuple-element.292, s32[1024]{0:T(1024)S(1)} %pad_clamp_fusion.4), kind=kCustom, calls=%fused_computation.clone.clone.1 | custom fusion | bytes 1048640 | tf_op jit(solution)/shard_map/while/body/eval_jaxpr/jit(_take)/gather | solution.py:103
  71.9 2.0 %gather_fusion = bf16[16,16,1024]{2,1,0:T(8,128)(2,1)S(1)} fusion(bf16[48,16,1024]{2,1,0:T(8,128)(2,1)} %get-tuple-element.292, s32[1024]{0:T(1024)S(1)} %pad_clamp_fusion.4), kind=kCustom, calls=%fused_computation.clone.clone.1 | custom fusion | bytes 1048640 | tf_op jit(solution)/shard_map/while/body/eval_jaxpr/jit(_take)/gather | solution.py:103
  74.9 2.0 %gather_fusion = bf16[16,16,1024]{2,1,0:T(8,128)(2,1)S(1)} fusion(bf16[48,16,1024]{2,1,0:T(8,128)(2,1)} %get-tuple-element.292, s32[1024]{0:T(1024)S(1)} %pad_clamp_fusion.4), kind=kCustom, calls=%fused_computation.clone.clone.1 | custom fusion | bytes 1048640 | tf_op jit(solution)/shard_map/while/body/eval_jaxpr/jit(_take)/gather | solution.py:103
  77.9 2.0 %gather_fusion = bf16[16,16,1024]{2,1,0:T(8,128)(2,1)S(1)} fusion(bf16[48,16,1024]{2,1,0:T(8,128)(2,1)} %get-tuple-element.292, s32[1024]{0:T(1024)S(1)} %pad_clamp_fusion.4), kind=kCustom, calls=%fused_computation.clone.clone.1 | custom fusion | bytes 1048640 | tf_op jit(solution)/shard_map/while/body/eval_jaxpr/jit(_take)/gather | solution.py:103
  80.9 2.0 %gather_fusion = bf16[16,16,1024]{2,1,0:T(8,128)(2,1)S(1)} fusion(bf16[48,16,1024]{2,1,0:T(8,128)(2,1)} %get-tuple-element.292, s32[1024]{0:T(1024)S(1)} %pad_clamp_fusion.4), kind=kCustom, calls=%fused_computation.clone.clone.1 | custom fusion | bytes 1048640 | tf_op jit(solution)/shard_map/while/body/eval_jaxpr/jit(_take)/gather | solution.py:103
  83.9 2.0 %gather_fusion = bf16[16,16,1024]{2,1,0:T(8,128)(2,1)S(1)} fusion(bf16[48,16,1024]{2,1,0:T(8,128)(2,1)} %get-tuple-element.292, s32[1024]{0:T(1024)S(1)} %pad_clamp_fusion.4), kind=kCustom, calls=%fused_computation.clone.clone.1 | custom fusion | bytes 1048640 | tf_op jit(solution)/shard_map/while/body/eval_jaxpr/jit(_take)/gather | solution.py:103
  90.0 2.0 %gather_fusion = bf16[16,16,1024]{2,1,0:T(8,128)(2,1)S(1)} fusion(bf16[48,16,1024]{2,1,0:T(8,128)(2,1)} %get-tuple-element.292, s32[1024]{0:T(1024)S(1)} %pad_clamp_fusion.4), kind=kCustom, calls=%fused_computation.clone.clone.1 | custom fusion | bytes 1048640 | tf_op jit(solution)/shard_map/while/body/eval_jaxpr/jit(_take)/gather | solution.py:103
  93.0 2.0 %gather_fusion = bf16[16,16,1024]{2,1,0:T(8,128)(2,1)S(1)} fusion(bf16[48,16,1024]{2,1,0:T(8,128)(2,1)} %get-tuple-element.292, s32[1024]{0:T(1024)S(1)} %pad_clamp_fusion.4), kind=kCustom, calls=%fused_computation.clone.clone.1 | custom fusion | bytes 1048640 | tf_op jit(solution)/shard_map/while/body/eval_jaxpr/jit(_take)/gather | solution.py:103
  96.0 2.0 %gather_fusion = bf16[16,16,1024]{2,1,0:T(8,128)(2,1)S(1)} fusion(bf16[48,16,1024]{2,1,0:T(8,128)(2,1)} %get-tuple-element.292, s32[1024]{0:T(1024)S(1)} %pad_clamp_fusion.4), kind=kCustom, calls=%fused_computation.clone.clone.1 | custom fusion | bytes 1048640 | tf_op jit(solution)/shard_map/while/body/eval_jaxpr/jit(_take)/gather | solution.py:103
  99.0 2.0 %gather_fusion = bf16[16,16,1024]{2,1,0:T(8,128)(2,1)S(1)} fusion(bf16[48,16,1024]{2,1,0:T(8,128)(2,1)} %get-tuple-element.292, s32[1024]{0:T(1024)S(1)} %pad_clamp_fusion.4), kind=kCustom, calls=%fused_computation.clone.clone.1 | custom fusion | bytes 1048640 | tf_op jit(solution)/shard_map/while/body/eval_jaxpr/jit(_take)/gather | solution.py:103
  105.0 2.0 %gather_fusion = bf16[16,16,1024]{2,1,0:T(8,128)(2,1)S(1)} fusion(bf16[48,16,1024]{2,1,0:T(8,128)(2,1)} %get-tuple-element.292, s32[1024]{0:T(1024)S(1)} %pad_clamp_fusion.4), kind=kCustom, calls=%fused_computation.clone.clone.1 | custom fusion | bytes 1048640 | tf_op jit(solution)/shard_map/while/body/eval_jaxpr/jit(_take)/gather | solution.py:103
  108.0 2.0 %gather_fusion = bf16[16,16,1024]{2,1,0:T(8,128)(2,1)S(1)} fusion(bf16[48,16,1024]{2,1,0:T(8,128)(2,1)} %get-tuple-element.292, s32[1024]{0:T(1024)S(1)} %pad_clamp_fusion.4), kind=kCustom, calls=%fused_computation.clone.clone.1 | custom fusion | bytes 1048640 | tf_op jit(solution)/shard_map/while/body/eval_jaxpr/jit(_take)/gather | solution.py:103
  111.0 2.0 %gather_fusion = bf16[16,16,1024]{2,1,0:T(8,128)(2,1)S(1)} fusion(bf16[48,16,1024]{2,1,0:T(8,128)(2,1)} %get-tuple-element.292, s32[1024]{0:T(1024)S(1)} %pad_clamp_fusion.4), kind=kCustom, calls=%fused_computation.clone.clone.1 | custom fusion | bytes 1048640 | tf_op jit(solution)/shard_map/while/body/eval_jaxpr/jit(_take)/gather | solution.py:103
  116.5 4.0 %fusion.19 = bf16[32,16,4,128]{3,2,1,0:T(4,128)(2,1)S(1)} fusion(f32[32,16,8,2,128]{4,1,3,0,2:T(8,128)S(1)} %convolution_bitcast_fusion, s32[8,2]{0,1:T(2,128)S(1)} %copy-done.9), kind=kOutput, calls=%fused_computation.29 | convolution fusion | flops 50593856 | bytes 4718656 | tf_op jit(solution)/shard_map/lcbri,brq->lcqi/dot_general | solution.py:129
  121.6 3.7 %collective-permute-start.2 = (bf16[4,8,128]{2,1,0:T(8,128)(2,1)S(1)}, bf16[4,8,128]{2,1,0:T(8,128)(2,1)S(1)}, u32[]{:S(2)}, u32[]{:S(2)}) collective-permute-start(bf16[4,8,128]{2,1,0:T(8,128)(2,1)S(1)} %copy-done.4), channel_id=1, source_target_pairs={{0,1},{1,2},{2,3},{3,4},{4,5},{5,6},{6,7},{7,8},{8,9},{9,10},{10,1... | collective-permute-start | bytes 24584 | tf_op jit(solution)/shard_map/ppermute | solution.py:17
  125.3 4.6 %collective-permute-start.3 = (bf16[4,8,128]{2,1,0:T(8,128)(2,1)S(1)}, bf16[4,8,128]{2,1,0:T(8,128)(2,1)S(1)}, u32[]{:S(2)}, u32[]{:S(2)}) collective-permute-start(bf16[4,8,128]{2,1,0:T(8,128)(2,1)S(1)} %copy-done.4), channel_id=1, source_target_pairs={{1,0},{2,1},{3,2},{4,3},{5,4},{6,5},{7,6},{8,7},{9,8},{10,9},{11,1... | collective-permute-start | bytes 24584 | tf_op jit(solution)/shard_map/ppermute | solution.py:19
  135.2 29.9 %reduce-scatter.2.cloned.1.call-done = bf16[4,16,512]{2,1,0:T(8,128)(2,1)} async-done(((bf16[32,16,512]{2,1,0:T(8,128)(2,1)}), bf16[4,16,512]{2,1,0:T(8,128)(2,1)}) %reduce-scatter.2.cloned.1.call-update) | async-done | bytes 65552 | tf_op jit(solution)/shard_map/reduce_scatter | solution.py:130
  (214 shorter events, 46.3 us)
Async XLA Ops:
  6.5 37.6 %copy-start = (bf16[8,2,128,128]{3,2,1,0:T(8,128)(2,1)S(1)}, bf16[8,2,128,128]{3,2,1,0:T(8,128)(2,1)}, u32[]{:S(2)}) copy-start(bf16[8,2,128,128]{3,2,1,0:T(8,128)(2,1)} %param.22) | copy-start | bytes 1572868
  6.5 3.7 %copy-start.4 = (bf16[4,8,128]{2,1,0:T(8,128)(2,1)S(1)}, bf16[4,8,128]{2,1,0:T(8,128)(2,1)}, u32[]{:S(2)}) copy-start(bf16[4,8,128]{2,1,0:T(8,128)(2,1)} %param.14) | copy-start | bytes 24580
  6.5 3.7 %copy-start.1 = (bf16[4,2,2,512,128]{4,3,2,1,0:T(8,128)(2,1)S(1)}, bf16[4,2,2,512,128]{4,3,2,1,0:T(8,128)(2,1)}, u32[]{:S(2)}) copy-start(bf16[4,2,2,512,128]{4,3,2,1,0:T(8,128)(2,1)} %param.15) | copy-start | bytes 6291460
  6.5 3.4 %copy-start.11 = (s32[32]{0:T(128)S(1)}, s32[32]{0:T(128)}, u32[]{:S(2)}) copy-start(s32[32]{0:T(128)} %param.19) | copy-start | bytes 388
  6.5 3.4 %copy-start.6 = (bf16[8,2,1024]{2,1,0:T(2,128)(2,1)S(1)}, bf16[8,2,1024]{2,1,0:T(2,128)(2,1)}, u32[]{:S(2)}) copy-start(bf16[8,2,1024]{2,1,0:T(2,128)(2,1)} %param.20) | copy-start | bytes 98308
  6.5 158.5 %reduce-scatter.2.cloned.1.call-start = ((), (), s32[]{:S(2)}) async-start(), calls=%async_computation.1 | async-start | bytes 589824 | tf_op jit(solution)/shard_map/reduce_scatter | solution.py:130
  10.3 32.6 %copy-start.9 = (s32[8,2]{0,1:T(2,128)S(1)}, s32[8,2]{0,1:T(2,128)}, u32[]{:S(2)}) copy-start(s32[8,2]{0,1:T(2,128)} %param.21) | copy-start | bytes 196
  47.4 1.7 copy-start.12
  49.5 6.7 %copy-start.5 = (bf16[32,2,1024]{2,1,0:T(2,128)(2,1)S(1)}, bf16[32,2,1024]{2,1,0:T(2,128)(2,1)}, u32[]{:S(2)}) copy-start(bf16[32,2,1024]{2,1,0:T(2,128)(2,1)} %param.25) | copy-start | bytes 393220
  49.5 6.7 %copy-start.7 = (s32[16,16]{1,0:T(8,128)S(1)}, s32[16,16]{1,0:T(8,128)}, u32[]{:S(2)}) copy-start(s32[16,16]{1,0:T(8,128)} %param.24) | copy-start | bytes 3076
  49.5 6.8 %copy-start.8 = (s32[16,16]{1,0:T(8,128)S(1)}, s32[16,16]{1,0:T(8,128)}, u32[]{:S(2)}) copy-start(s32[16,16]{1,0:T(8,128)} %param.23) | copy-start | bytes 3076
  50.4 10.5 %collective-permute-start = (bf16[16,16,1024]{2,0,1:T(8,128)(2,1)S(1)}, bf16[16,16,1024]{2,0,1:T(8,128)(2,1)S(1)}, u32[]{:S(2)}, u32[]{:S(2)}) collective-permute-start(bf16[16,16,1024]{2,0,1:T(8,128)(2,1)S(1)} %fusion.16), channel_id=1, source_target_pairs={{0,8},{8,16},{16,24},{24,32},{32,40},{40,48},{48,56},{56,64},{64,7... | collective-permute-start | bytes 1572872 | tf_op jit(solution)/shard_map/ppermute | solution.py:17
  52.3 10.3 %collective-permute-start.1 = (bf16[16,16,1024]{2,0,1:T(8,128)(2,1)S(1)}, bf16[16,16,1024]{2,0,1:T(8,128)(2,1)}, u32[]{:S(2)}, u32[]{:S(2)}) collective-permute-start(bf16[16,16,1024]{2,0,1:T(8,128)(2,1)S(1)} %fusion.16), channel_id=1, source_target_pairs={{8,0},{16,8},{24,16},{32,24},{40,32},{48,40},{56,48},{64,56},{72,6... | collective-permute-start | bytes 1572872 | tf_op jit(solution)/shard_map/ppermute | solution.py:19
  116.5 13.4 %copy-start.10 = (s32[4,8]{1,0:T(4,128)S(1)}, s32[4,8]{1,0:T(4,128)}, u32[]{:S(2)}) copy-start(s32[4,8]{1,0:T(4,128)} %param.17) | copy-start | bytes 388
  120.6 45.3 %copy-start.2 = (bf16[4,2,2,512,128]{4,3,2,1,0:T(8,128)(2,1)S(1)}, bf16[4,2,2,512,128]{4,3,2,1,0:T(8,128)(2,1)}, u32[]{:S(2)}) copy-start(bf16[4,2,2,512,128]{4,3,2,1,0:T(8,128)(2,1)} %param.15) | copy-start | bytes 6291460
  121.6 8.4 %collective-permute-start.2 = (bf16[4,8,128]{2,1,0:T(8,128)(2,1)S(1)}, bf16[4,8,128]{2,1,0:T(8,128)(2,1)S(1)}, u32[]{:S(2)}, u32[]{:S(2)}) collective-permute-start(bf16[4,8,128]{2,1,0:T(8,128)(2,1)S(1)} %copy-done.4), channel_id=1, source_target_pairs={{0,1},{1,2},{2,3},{3,4},{4,5},{5,6},{6,7},{7,8},{8,9},{9,10},{10,1... | collective-permute-start | bytes 24584 | tf_op jit(solution)/shard_map/ppermute | solution.py:17
  125.3 5.9 %collective-permute-start.3 = (bf16[4,8,128]{2,1,0:T(8,128)(2,1)S(1)}, bf16[4,8,128]{2,1,0:T(8,128)(2,1)S(1)}, u32[]{:S(2)}, u32[]{:S(2)}) collective-permute-start(bf16[4,8,128]{2,1,0:T(8,128)(2,1)S(1)} %copy-done.4), channel_id=1, source_target_pairs={{1,0},{2,1},{3,2},{4,3},{5,4},{6,5},{7,6},{8,7},{9,8},{10,9},{11,1... | collective-permute-start | bytes 24584 | tf_op jit(solution)/shard_map/ppermute | solution.py:19
  166.1 1.6 copy-start.3
Sparse Core Ops, SparseCore 0:
  121.7 43.2 reduce-scatter.1
where the time goes:
time: 177 us; the launch traced here: 176 us
  local copies, waits for them, and re-layouts  44.3 us (25%)
  waiting for transfers between devices  37.4 us (21%)
  blocking collectives  31.6 us (18%)
  matrix products  19.5 us (11%)
  other arithmetic  14.1 us (8%)
  starting transfers between devices  14 us (8%)
  between operations  13.8 us (8%)
    gather x16, local copies, waits for them, and re-layouts, add_entry(): jnp.take(padded, top_src[:, entry] - base_index, axis=0).astype(jnp.float32)  31.8 us
    all_gather x1, blocking collectives, per_device(): piece = lax.all_gather(patterns, 'samp', axis=0, tiled=True)  31.6 us
    reduce_scatter x1, waiting for transfers between devices, per_device(): lax.psum_scatter(folded.reshape(leaf_count * lax.axis_size('samp'), comps...  29.9 us
    dot_general x32, matrix products, contract(): jnp.einsum(form, first_op, second_op, preferred_element_type=jnp.float32)  14.6 us
    ppermute x2, starting transfers between devices, with_halo(): lax.ppermute(head, axis, [((i + 1) % count, i) for i in range(ends)])  8.4 us
    ppermute x2, starting transfers between devices, with_halo(): lax.ppermute(tail, axis, [(i, (i + 1) % count) for i in range(ends)])  5.61 us
    add x16, other arithmetic, add_entry(): return total + jnp.concatenate([part_real, part_imag], axis=1)  5.52 us
    ppermute x2, waiting for transfers between devices, with_halo(): lax.ppermute(tail, axis, [(i, (i + 1) % count) for i in range(ends)])  4.53 us
  transfers between devices with their start and end apart: 5, of which 4 were waited for; matrix products, arithmetic and copies ran while one was open for 2% of the time, Pallas kernels for 0%

commit v1 on v0

--- a/solution.py
+++ b/solution.py
@@ -4,6 +4,14 @@
 from jax.sharding import PartitionSpec as P
 
 HIGHEST = lax.Precision.HIGHEST
+
+
+def save_paths(x_part):
+    f_now = lax.psum(1, axis_name="samp")
+    return jnp.concatenate(
+        lax.all_to_all(jnp.stack(f_now * [x_part]), axis_name="samp", split_axis=0, concat_axis=0),
+        axis=0,
+    )
 
 
 def with_halo(cells, sides, width):
@@ -75,7 +83,7 @@
         ],
         axis=1,
     ).astype(jnp.bfloat16)
-    piece = lax.all_gather(patterns, "samp", axis=0, tiled=True)
+    piece = save_paths(patterns)
     piece_rows = piece.shape[0]
     picked = piece.reshape(piece_rows, comps, in_blocks, block_size)[:, :, interp_idx, :]
     moved_rows = contract("lcbri,brki->lcbk", picked, interp_val)

time: 177 us -> 172 us (0.972)
  blocking collectives: 31.6 us -> 0 us
  waiting for transfers between devices: 37.4 us -> 52.1 us
  starting transfers between devices: 14 us -> 23.8 us
    all_gather x1 -> x0, blocking collectives: 31.6 us -> none  [per_device(): piece = lax.all_gather(patterns, 'samp', axis=0, tiled=True)]
    all_to_all x0 -> x1, waiting for transfers between devices: none -> 16.5 us  [save_paths(): lax.all_to_all(jnp.stack(f_now * [x_part]), axis_name='samp', split_axis=...]
    all_to_all x0 -> x1, starting transfers between devices: none -> 10.3 us  [save_paths(): lax.all_to_all(jnp.stack(f_now * [x_part]), axis_name='samp', split_axis=...]
    unnamed x32 -> x34, local copies, waits for them, and re-layouts: 3.28 us -> 3.62 us
  transfers between devices with their start and end apart: 5 -> 6, of which waited for: 4 -> 5; matrix products, arithmetic and copies ran while one was open for 2% -> 3% of each run, Pallas kernels for 0% -> 0%
where the time goes in v1:
time: 172 us; the launch traced here: 171 us
  waiting for transfers between devices  52.1 us (30%)
  local copies, waits for them, and re-layouts  45.7 us (27%)
  starting transfers between devices  23.8 us (14%)
  matrix products  19.4 us (11%)
  other arithmetic  14.6 us (8%)
  between operations  13.8 us (8%)
    gather x16, local copies, waits for them, and re-layouts, add_entry(): jnp.take(padded, top_src[:, entry] - base_index, axis=0).astype(jnp.float32)  31.8 us
    reduce_scatter x1, waiting for transfers between devices, per_device(): lax.psum_scatter(folded.reshape(leaf_count * lax.axis_size('samp'), comps...  28.1 us
    all_to_all x1, waiting for transfers between devices, save_paths(): lax.all_to_all(jnp.stack(f_now * [x_part]), axis_name='samp', split_axis=...  16.5 us
    dot_general x32, matrix products, contract(): jnp.einsum(form, first_op, second_op, preferred_element_type=jnp.float32)  14.6 us
    all_to_all x1, starting transfers between devices, save_paths(): lax.all_to_all(jnp.stack(f_now * [x_part]), axis_name='samp', split_axis=...  10.3 us
    ppermute x2, starting transfers between devices, with_halo(): lax.ppermute(head, axis, [((i + 1) % count, i) for i in range(ends)])  9.01 us
    add x16, other arithmetic, add_entry(): return total + jnp.concatenate([part_real, part_imag], axis=1)  5.52 us
    ppermute x2, waiting for transfers between devices, with_halo(): lax.ppermute(tail, axis, [(i, (i + 1) % count) for i in range(ends)])  4.53 us
  transfers between devices with their start and end apart: 6, of which 5 were waited for; matrix products, arithmetic and copies ran while one was open for 3% of the time, Pallas kernels for 0%

profile of v1, /device:TPU:2, one launch (start us, length us, event | category | flops | bytes accessed | tf_op | source)
XLA Modules:
  0.0 170.6 jit_solution(17930255361013981896)
XLA Ops:
  11.7 10.3 %all-to-all-start = ((bf16[8,4,16,512]{3,2,1,0:T(8,128)(2,1)}), bf16[8,4,16,512]{3,2,1,0:T(8,128)(2,1)S(1)}, u32[]{:S(2)}, u32[]{:S(2)}) async-start(bf16[8,4,16,512]{3,2,1,0:T(8,128)(2,1)} %stack.2), calls=%async_computation | async-start | bytes 1048576 | tf_op jit(solution)/shard_map/all_to_all | solution.py:12
  23.1 16.5 %all-to-all-done = bf16[8,4,16,512]{3,2,1,0:T(8,128)(2,1)S(1)} async-done(((bf16[8,4,16,512]{3,2,1,0:T(8,128)(2,1)}), bf16[8,4,16,512]{3,2,1,0:T(8,128)(2,1)S(1)}, u32[]{:S(2)}, u32[]{:S(2)}) %all-to-all-start) | async-done | bytes 524320 | tf_op jit(solution)/shard_map/all_to_all | solution.py:12
  41.5 2.6 %copy.73 = f32[32,16,8,128]{3,2,0,1:T(8,128)} copy(f32[32,16,8,128]{3,1,0,2:T(8,128)S(1)} %convolution_bitcast_fusion.1) | data formatting | bytes 4194304 | tf_op jit(solution)/shard_map/reshape | solution.py:90
  49.2 3.8 %collective-permute-start.1 = (bf16[16,16,1024]{2,0,1:T(8,128)(2,1)S(1)}, bf16[16,16,1024]{2,0,1:T(8,128)(2,1)}, u32[]{:S(2)}, u32[]{:S(2)}) collective-permute-start(bf16[16,16,1024]{2,0,1:T(8,128)(2,1)S(1)} %fusion.16), channel_id=1, source_target_pairs={{8,0},{16,8},{24,16},{32,24},{40,32},{48,40},{56,48},{64,56},{72,6... | collective-permute-start | bytes 1572872 | tf_op jit(solution)/shard_map/ppermute | solution.py:27
  53.3 4.5 %collective-permute-done = bf16[16,16,1024]{2,0,1:T(8,128)(2,1)S(1)} collective-permute-done((bf16[16,16,1024]{2,0,1:T(8,128)(2,1)S(1)}, bf16[16,16,1024]{2,0,1:T(8,128)(2,1)S(1)}, u32[]{:S(2)}, u32[]{:S(2)}) %collective-permute-start) | collective-permute-done | bytes 524320 | tf_op jit(solution)/shard_map/ppermute | solution.py:25
  60.8 2.1 %copy.51 = bf16[48,16,1024]{2,1,0:T(8,128)(2,1)} copy(bf16[48,16,1024]{2,0,1:T(8,128)(2,1)S(1)} %pad_maximum_fusion) | data formatting | bytes 3145728
  62.8 48.1 %while.14 = (s32[]{:T(128)}, f32[16,16,1024]{2,1,0:T(8,128)S(1)}, s32[16,16]{0,1:T(8,128)S(1)}, bf16[32,2,1024]{2,0,1:T(8,128)(2,1)S(1)}, s32[16,16]{0,1:T(8,128...) while((s32[]{:T(128)}, f32[16,16,1024]{2,1,0:T(8,128)S(1)}, ...), condition=%wide.region_1.0_spmd.clone, body=%wide.region_0.1_spmd.clone.sunk | while | flops 4195955 | bytes 8524371 | solution.py:121
  62.9 2.0 %gather_fusion = bf16[16,16,1024]{2,1,0:T(8,128)(2,1)S(1)} fusion(bf16[48,16,1024]{2,1,0:T(8,128)(2,1)} %get-tuple-element.285, s32[1024]{0:T(1024)S(1)} %pad_clamp_fusion.4), kind=kCustom, calls=%fused_computation.clone.clone.1 | custom fusion | bytes 1048640 | tf_op jit(solution)/shard_map/while/body/eval_jaxpr/jit(_take)/gather | solution.py:111
  65.9 2.0 %gather_fusion = bf16[16,16,1024]{2,1,0:T(8,128)(2,1)S(1)} fusion(bf16[48,16,1024]{2,1,0:T(8,128)(2,1)} %get-tuple-element.285, s32[1024]{0:T(1024)S(1)} %pad_clamp_fusion.4), kind=kCustom, calls=%fused_computation.clone.clone.1 | custom fusion | bytes 1048640 | tf_op jit(solution)/shard_map/while/body/eval_jaxpr/jit(_take)/gather | solution.py:111
  68.9 2.0 %gather_fusion = bf16[16,16,1024]{2,1,0:T(8,128)(2,1)S(1)} fusion(bf16[48,16,1024]{2,1,0:T(8,128)(2,1)} %get-tuple-element.285, s32[1024]{0:T(1024)S(1)} %pad_clamp_fusion.4), kind=kCustom, calls=%fused_computation.clone.clone.1 | custom fusion | bytes 1048640 | tf_op jit(solution)/shard_map/while/body/eval_jaxpr/jit(_take)/gather | solution.py:111
  71.9 2.0 %gather_fusion = bf16[16,16,1024]{2,1,0:T(8,128)(2,1)S(1)} fusion(bf16[48,16,1024]{2,1,0:T(8,128)(2,1)} %get-tuple-element.285, s32[1024]{0:T(1024)S(1)} %pad_clamp_fusion.4), kind=kCustom, calls=%fused_computation.clone.clone.1 | custom fusion | bytes 1048640 | tf_op jit(solution)/shard_map/while/body/eval_jaxpr/jit(_take)/gather | solution.py:111
  74.9 2.0 %gather_fusion = bf16[16,16,1024]{2,1,0:T(8,128)(2,1)S(1)} fusion(bf16[48,16,1024]{2,1,0:T(8,128)(2,1)} %get-tuple-element.285, s32[1024]{0:T(1024)S(1)} %pad_clamp_fusion.4), kind=kCustom, calls=%fused_computation.clone.clone.1 | custom fusion | bytes 1048640 | tf_op jit(solution)/shard_map/while/body/eval_jaxpr/jit(_take)/gather | solution.py:111
  77.9 2.0 %gather_fusion = bf16[16,16,1024]{2,1,0:T(8,128)(2,1)S(1)} fusion(bf16[48,16,1024]{2,1,0:T(8,128)(2,1)} %get-tuple-element.285, s32[1024]{0:T(1024)S(1)} %pad_clamp_fusion.4), kind=kCustom, calls=%fused_computation.clone.clone.1 | custom fusion | bytes 1048640 | tf_op jit(solution)/shard_map/while/body/eval_jaxpr/jit(_take)/gather | solution.py:111
  80.9 2.0 %gather_fusion = bf16[16,16,1024]{2,1,0:T(8,128)(2,1)S(1)} fusion(bf16[48,16,1024]{2,1,0:T(8,128)(2,1)} %get-tuple-element.285, s32[1024]{0:T(1024)S(1)} %pad_clamp_fusion.4), kind=kCustom, calls=%fused_computation.clone.clone.1 | custom fusion | bytes 1048640 | tf_op jit(solution)/shard_map/while/body/eval_jaxpr/jit(_take)/gather | solution.py:111
  83.9 2.0 %gather_fusion = bf16[16,16,1024]{2,1,0:T(8,128)(2,1)S(1)} fusion(bf16[48,16,1024]{2,1,0:T(8,128)(2,1)} %get-tuple-element.285, s32[1024]{0:T(1024)S(1)} %pad_clamp_fusion.4), kind=kCustom, calls=%fused_computation.clone.clone.1 | custom fusion | bytes 1048640 | tf_op jit(solution)/shard_map/while/body/eval_jaxpr/jit(_take)/gather | solution.py:111
  92.9 2.0 %gather_fusion = bf16[16,16,1024]{2,1,0:T(8,128)(2,1)S(1)} fusion(bf16[48,16,1024]{2,1,0:T(8,128)(2,1)} %get-tuple-element.285, s32[1024]{0:T(1024)S(1)} %pad_clamp_fusion.4), kind=kCustom, calls=%fused_computation.clone.clone.1 | custom fusion | bytes 1048640 | tf_op jit(solution)/shard_map/while/body/eval_jaxpr/jit(_take)/gather | solution.py:111
  95.9 2.0 %gather_fusion = bf16[16,16,1024]{2,1,0:T(8,128)(2,1)S(1)} fusion(bf16[48,16,1024]{2,1,0:T(8,128)(2,1)} %get-tuple-element.285, s32[1024]{0:T(1024)S(1)} %pad_clamp_fusion.4), kind=kCustom, calls=%fused_computation.clone.clone.1 | custom fusion | bytes 1048640 | tf_op jit(solution)/shard_map/while/body/eval_jaxpr/jit(_take)/gather | solution.py:111
  98.9 2.0 %gather_fusion = bf16[16,16,1024]{2,1,0:T(8,128)(2,1)S(1)} fusion(bf16[48,16,1024]{2,1,0:T(8,128)(2,1)} %get-tuple-element.285, s32[1024]{0:T(1024)S(1)} %pad_clamp_fusion.4), kind=kCustom, calls=%fused_computation.clone.clone.1 | custom fusion | bytes 1048640 | tf_op jit(solution)/shard_map/while/body/eval_jaxpr/jit(_take)/gather | solution.py:111
  105.0 2.0 %gather_fusion = bf16[16,16,1024]{2,1,0:T(8,128)(2,1)S(1)} fusion(bf16[48,16,1024]{2,1,0:T(8,128)(2,1)} %get-tuple-element.285, s32[1024]{0:T(1024)S(1)} %pad_clamp_fusion.4), kind=kCustom, calls=%fused_computation.clone.clone.1 | custom fusion | bytes 1048640 | tf_op jit(solution)/shard_map/while/body/eval_jaxpr/jit(_take)/gather | solution.py:111
  108.0 2.0 %gather_fusion = bf16[16,16,1024]{2,1,0:T(8,128)(2,1)S(1)} fusion(bf16[48,16,1024]{2,1,0:T(8,128)(2,1)} %get-tuple-element.285, s32[1024]{0:T(1024)S(1)} %pad_clamp_fusion.4), kind=kCustom, calls=%fused_computation.clone.clone.1 | custom fusion | bytes 1048640 | tf_op jit(solution)/shard_map/while/body/eval_jaxpr/jit(_take)/gather | solution.py:111
  113.5 4.0 %fusion.19 = bf16[32,16,4,128]{3,2,1,0:T(4,128)(2,1)S(1)} fusion(f32[32,16,8,2,128]{4,1,3,0,2:T(8,128)S(1)} %convolution_bitcast_fusion, s32[8,2]{0,1:T(2,128)S(1)} %copy-done.9), kind=kOutput, calls=%fused_computation.29 | convolution fusion | flops 50593856 | bytes 4718656 | tf_op jit(solution)/shard_map/lcbri,brq->lcqi/dot_general | solution.py:137
  118.6 2.5 %collective-permute-start.2 = (bf16[4,8,128]{2,1,0:T(8,128)(2,1)S(1)}, bf16[4,8,128]{2,1,0:T(8,128)(2,1)S(1)}, u32[]{:S(2)}, u32[]{:S(2)}) collective-permute-start(bf16[4,8,128]{2,1,0:T(8,128)(2,1)S(1)} %copy-done.4), channel_id=1, source_target_pairs={{0,1},{1,2},{2,3},{3,4},{4,5},{5,6},{6,7},{7,8},{8,9},{9,10},{10,1... | collective-permute-start | bytes 24584 | tf_op jit(solution)/shard_map/ppermute | solution.py:25
  121.1 5.2 %collective-permute-start.3 = (bf16[4,8,128]{2,1,0:T(8,128)(2,1)S(1)}, bf16[4,8,128]{2,1,0:T(8,128)(2,1)S(1)}, u32[]{:S(2)}, u32[]{:S(2)}) collective-permute-start(bf16[4,8,128]{2,1,0:T(8,128)(2,1)S(1)} %copy-done.4), channel_id=1, source_target_pairs={{1,0},{2,1},{3,2},{4,3},{5,4},{6,5},{7,6},{8,7},{9,8},{10,9},{11,1... | collective-permute-start | bytes 24584 | tf_op jit(solution)/shard_map/ppermute | solution.py:27
  131.5 28.1 %reduce-scatter.2.cloned.1.call-done = bf16[4,16,512]{2,1,0:T(8,128)(2,1)} async-done(((bf16[32,16,512]{2,1,0:T(8,128)(2,1)}), bf16[4,16,512]{2,1,0:T(8,128)(2,1)}) %reduce-scatter.2.cloned.1.call-update) | async-done | bytes 65552 | tf_op jit(solution)/shard_map/reduce_scatter | solution.py:138
  (219 shorter events, 50.1 us)
Async XLA Ops:
  6.5 34.3 %copy-start = (bf16[8,2,128,128]{3,2,1,0:T(8,128)(2,1)S(1)}, bf16[8,2,128,128]{3,2,1,0:T(8,128)(2,1)}, u32[]{:S(2)}) copy-start(bf16[8,2,128,128]{3,2,1,0:T(8,128)(2,1)} %param.22) | copy-start | bytes 1572868
  6.5 3.4 %copy-start.4 = (bf16[4,8,128]{2,1,0:T(8,128)(2,1)S(1)}, bf16[4,8,128]{2,1,0:T(8,128)(2,1)}, u32[]{:S(2)}) copy-start(bf16[4,8,128]{2,1,0:T(8,128)(2,1)} %param.14) | copy-start | bytes 24580
  6.5 3.4 %copy-start.1 = (bf16[4,2,2,512,128]{4,3,2,1,0:T(8,128)(2,1)S(1)}, bf16[4,2,2,512,128]{4,3,2,1,0:T(8,128)(2,1)}, u32[]{:S(2)}) copy-start(bf16[4,2,2,512,128]{4,3,2,1,0:T(8,128)(2,1)} %param.15) | copy-start | bytes 6291460
  9.9 12.1 %copy-start.9 = (s32[8,2]{0,1:T(2,128)S(1)}, s32[8,2]{0,1:T(2,128)}, u32[]{:S(2)}) copy-start(s32[8,2]{0,1:T(2,128)} %param.21) | copy-start | bytes 196
  10.0 12.3 %copy-start.13 = (s32[32]{0:T(128)S(1)}, s32[32]{0:T(128)}, u32[]{:S(2)}) copy-start(s32[32]{0:T(128)} %param.18) | copy-start | bytes 388
  10.0 12.8 %copy-start.6 = (bf16[8,2,1024]{2,1,0:T(2,128)(2,1)S(1)}, bf16[8,2,1024]{2,1,0:T(2,128)(2,1)}, u32[]{:S(2)}) copy-start(bf16[8,2,1024]{2,1,0:T(2,128)(2,1)} %param.20) | copy-start | bytes 98308
  10.0 12.8 %copy-start.12 = (s32[32]{0:T(128)S(1)}, s32[32]{0:T(128)}, u32[]{:S(2)}) copy-start(s32[32]{0:T(128)} %param.19) | copy-start | bytes 388
  11.7 27.8 %all-to-all-start = ((bf16[8,4,16,512]{3,2,1,0:T(8,128)(2,1)}), bf16[8,4,16,512]{3,2,1,0:T(8,128)(2,1)S(1)}, u32[]{:S(2)}, u32[]{:S(2)}) async-start(bf16[8,4,16,512]{3,2,1,0:T(8,128)(2,1)} %stack.2), calls=%async_computation | async-start | bytes 1048576 | tf_op jit(solution)/shard_map/all_to_all | solution.py:12
  22.0 137.6 %reduce-scatter.2.cloned.1.call-start = ((), (), s32[]{:S(2)}) async-start(), calls=%async_computation.2 | async-start | bytes 589824 | tf_op jit(solution)/shard_map/reduce_scatter | solution.py:138
  45.8 0.7 copy-start.11
  46.1 7.0 %copy-start.5 = (bf16[32,2,1024]{2,1,0:T(2,128)(2,1)S(1)}, bf16[32,2,1024]{2,1,0:T(2,128)(2,1)}, u32[]{:S(2)}) copy-start(bf16[32,2,1024]{2,1,0:T(2,128)(2,1)} %param.25) | copy-start | bytes 393220
  46.1 7.0 %copy-start.7 = (s32[16,16]{1,0:T(8,128)S(1)}, s32[16,16]{1,0:T(8,128)}, u32[]{:S(2)}) copy-start(s32[16,16]{1,0:T(8,128)} %param.24) | copy-start | bytes 3076
  46.2 7.1 %copy-start.8 = (s32[16,16]{1,0:T(8,128)S(1)}, s32[16,16]{1,0:T(8,128)}, u32[]{:S(2)}) copy-start(s32[16,16]{1,0:T(8,128)} %param.23) | copy-start | bytes 3076
  47.3 10.5 %collective-permute-start = (bf16[16,16,1024]{2,0,1:T(8,128)(2,1)S(1)}, bf16[16,16,1024]{2,0,1:T(8,128)(2,1)S(1)}, u32[]{:S(2)}, u32[]{:S(2)}) collective-permute-start(bf16[16,16,1024]{2,0,1:T(8,128)(2,1)S(1)} %fusion.16), channel_id=1, source_target_pairs={{0,8},{8,16},{16,24},{24,32},{32,40},{40,48},{48,56},{56,64},{64,7... | collective-permute-start | bytes 1572872 | tf_op jit(solution)/shard_map/ppermute | solution.py:25
  49.2 10.3 %collective-permute-start.1 = (bf16[16,16,1024]{2,0,1:T(8,128)(2,1)S(1)}, bf16[16,16,1024]{2,0,1:T(8,128)(2,1)}, u32[]{:S(2)}, u32[]{:S(2)}) collective-permute-start(bf16[16,16,1024]{2,0,1:T(8,128)(2,1)S(1)} %fusion.16), channel_id=1, source_target_pairs={{8,0},{16,8},{24,16},{32,24},{40,32},{48,40},{56,48},{64,56},{72,6... | collective-permute-start | bytes 1572872 | tf_op jit(solution)/shard_map/ppermute | solution.py:27
  113.5 12.8 %copy-start.10 = (s32[4,8]{1,0:T(4,128)S(1)}, s32[4,8]{1,0:T(4,128)}, u32[]{:S(2)}) copy-start(s32[4,8]{1,0:T(4,128)} %param.17) | copy-start | bytes 388
  117.5 42.9 %copy-start.2 = (bf16[4,2,2,512,128]{4,3,2,1,0:T(8,128)(2,1)S(1)}, bf16[4,2,2,512,128]{4,3,2,1,0:T(8,128)(2,1)}, u32[]{:S(2)}) copy-start(bf16[4,2,2,512,128]{4,3,2,1,0:T(8,128)(2,1)} %param.15) | copy-start | bytes 6291460
  118.6 7.8 %collective-permute-start.2 = (bf16[4,8,128]{2,1,0:T(8,128)(2,1)S(1)}, bf16[4,8,128]{2,1,0:T(8,128)(2,1)S(1)}, u32[]{:S(2)}, u32[]{:S(2)}) collective-permute-start(bf16[4,8,128]{2,1,0:T(8,128)(2,1)S(1)} %copy-done.4), channel_id=1, source_target_pairs={{0,1},{1,2},{2,3},{3,4},{4,5},{5,6},{6,7},{7,8},{8,9},{9,10},{10,1... | collective-permute-start | bytes 24584 | tf_op jit(solution)/shard_map/ppermute | solution.py:25
  121.1 6.5 %collective-permute-start.3 = (bf16[4,8,128]{2,1,0:T(8,128)(2,1)S(1)}, bf16[4,8,128]{2,1,0:T(8,128)(2,1)S(1)}, u32[]{:S(2)}, u32[]{:S(2)}) collective-permute-start(bf16[4,8,128]{2,1,0:T(8,128)(2,1)S(1)} %copy-done.4), channel_id=1, source_target_pairs={{1,0},{2,1},{3,2},{4,3},{5,4},{6,5},{7,6},{8,7},{9,8},{10,9},{11,1... | collective-permute-start | bytes 24584 | tf_op jit(solution)/shard_map/ppermute | solution.py:27
  160.7 1.6 copy-start.3
Sparse Core Ops, SparseCore 0:
  118.7 40.9 reduce-scatter.1
